TPU v7x, 128 devices: a whole 4x4x4 slice. The times are simulated.
128 devices in a mesh: row: 8 (over y, core), col: 16 (over z, x).
Axes of the slice: x: 4, y: 4, z: 4, core: 2. Of those that a mesh axis runs over, the one named last changes fastest.
Arguments:
- wavefield: bfloat16 [65536, 2, 128], P(('col', 'row')), may hold values from -6 to 6
- recorded: bfloat16 [65536, 2, 128], P(('row', 'col')), may hold values from -6 to 6
- v_bases: bfloat16 [256, 256, 32, 256], P('row', 'col'), may hold values from -0.25 to 0.25
- u_bases: bfloat16 [256, 256, 32, 256], P(('row', 'col')), may hold values from -0.0625 to 0.0625
- ranks: int32 [256, 256], P('row', 'col'), may hold values from 1 to 16
Outputs:
- residual: float32 [65536, 2, 128], P(('row', 'col'))
- gradient: float32 [65536, 2, 128], P(('col', 'row'))
Inputs may be any that keep to these rules, and one draw needn't show every extreme that they name: `ranks`: some tile has rank 16.
All inputs are finite; a program needn't handle non-finite values.
Results may differ from a plain program's by a relative error of at most 0.0038.
Values may be sent and summed in bfloat16 or wider, within the bound.
No kernel may reach another device: no remote copies, remote signals or barrier semaphores. Data moves between devices by JAX's collectives and lax.ppermute only.
A program may use at most 128 MiB of HBM per device.

v0:
```python
import jax
import jax.numpy as jnp
from jax import lax
from jax.sharding import PartitionSpec as P


def combine_adjoint(prod):
    half = prod.shape[2] // 2
    real = prod[:, :, :half, 0] + prod[:, :, half:, 1]
    imag = prod[:, :, :half, 1] - prod[:, :, half:, 0]
    return jnp.stack([real, imag], axis=3)


def stacked(coeffs):
    real = coeffs[:, :, :, 0]
    imag = coeffs[:, :, :, 1]
    first = jnp.concatenate([real, -imag], axis=2)
    second = jnp.concatenate([imag, real], axis=2)
    return jnp.stack([first, second], axis=3)


def v_adjoint(bases, blocks, mask):
    prod = jnp.einsum("ijrk,jkcs->ijrcs", bases, blocks, preferred_element_type=jnp.float32)
    return (combine_adjoint(prod) * mask[:, :, :, None, None]).astype(jnp.bfloat16)


def u_apply(bases, coeffs):
    return jnp.einsum(
        "ijrk,ijrcs->ikcs", bases, stacked(coeffs), preferred_element_type=jnp.float32
    )


def u_adjoint(bases, rows):
    prod = jnp.einsum("ijrk,ikcs->ijrcs", bases, rows, preferred_element_type=jnp.float32)
    return combine_adjoint(prod).astype(jnp.bfloat16)


def v_apply(bases, back, mask):
    masked = back * mask.astype(jnp.bfloat16)[:, :, :, None, None]
    return jnp.einsum(
        "ijrk,ijrcs->jkcs", bases, stacked(masked), preferred_element_type=jnp.float32
    )


def body(wavefield, recorded, v_bases, u_bases, ranks):
    tile = v_bases.shape[3]
    rank = v_bases.shape[2] // 2
    sources = wavefield.shape[2]
    levels = lax.broadcasted_iota(jnp.int32, (ranks.shape[0], ranks.shape[1], rank), 2)
    mask = (levels < ranks[:, :, None]).astype(jnp.float32)
    gathered = lax.all_gather(wavefield, "row", axis=0, tiled=True)
    blocks = gathered.reshape(-1, tile, 2, sources)
    coeffs = v_adjoint(v_bases, blocks, mask)
    local_left = lax.all_to_all(u_bases, "col", split_axis=1, concat_axis=0, tiled=True)
    partial_value = u_apply(local_left, coeffs).reshape(-1, 2, sources)
    modelled = lax.psum_scatter(partial_value, "col", scatter_dimension=0, tiled=True)
    residual = modelled - recorded.astype(jnp.float32)
    rounded = residual.astype(jnp.bfloat16)
    whole_rows = lax.all_gather(rounded, "col", axis=0, tiled=True).reshape(-1, tile, 2, sources)
    back = u_adjoint(local_left, whole_rows)
    column_terms = v_apply(v_bases, back, mask)
    gradient = lax.psum_scatter(
        column_terms.reshape(-1, 2, sources), "row", scatter_dimension=0, tiled=True
    )
    return (residual, gradient)


def solution(mesh):
    in_specs = (
        P(("col", "row"), None, None),
        P(("row", "col"), None, None),
        P("row", "col", None, None),
        P(("row", "col"), None, None, None),
        P("row", "col"),
    )
    out_specs = (P(("row", "col"), None, None), P(("col", "row"), None, None))
    return jax.shard_map(body, mesh=mesh, in_specs=in_specs, out_specs=out_specs, check_vma=False)
```

profile of v0, /device:TPU:0, one launch (start us, length us, event | category | flops | bytes accessed | tf_op | source)
XLA Modules:
  0.0 404.6 jit_solution(17005958906156054134)
XLA Ops:
  7.2 8.1 %copy.35 = bf16[2,256,32,256]{3,2,0,1:T(8,128)(2,1)} copy(bf16[2,256,32,256]{3,2,1,0:T(8,128)(2,1)} %param.8) | data formatting | bytes 16777216 | tf_op args[3]
  15.2 8.2 %all-to-all-start = ((bf16[2,256,32,256]{3,2,0,1:T(8,128)(2,1)}), bf16[2,256,32,256]{3,2,0,1:T(8,128)(2,1)}, u32[]{:S(2)}, u32[]{:S(2)}) async-start(bf16[2,256,32,256]{3,2,0,1:T(8,128)(2,1)} %copy.35), calls=%async_computation | async-start | bytes 16777216 | tf_op jit(solution)/shard_map/all_to_all | solution.py:54
  24.4 29.1 %all-gather.3.cloned.1.call-done = bf16[4096,2,128]{2,0,1:T(8,128)(2,1)} async-done(((bf16[512,2,128]{2,0,1:T(8,128)(2,1)}), bf16[4096,2,128]{2,0,1:T(8,128)(2,1)}) %all-gather.3.cloned.1.call-update) | async-done | bytes 2097168 | tf_op jit(solution)/shard_map/all_gather | solution.py:51
  53.5 12.1 %convolution_bitcast_fusion.1 = f32[32,16,32,2,128]{4,2,0,3,1:T(8,128)} fusion(bf16[16,256,2,128,1]{3,1,0,2,4:T(8,128)(2,1)} %bitcast.69, bf16[32,16,32,256]{3,2,1,0:T(8,128)(2,1)} %param.7), kind=kOutput, calls=%fused_computation.1 | convolution fusion | flops 2147483648 | bytes 27262976 | tf_op jit(solution)/shard_map/ijrk,jkcs->ijrcs/dot_general | solution.py:23
  65.6 9.4 %slice_add_fusion.1 = (f32[32,16,16,1,128]{4,2,0,3,1:T(8,128)S(1)}, f32[32,16,16,1,128]{4,2,0,3,1:T(8,128)}) fusion(f32[32,16,32,2,128]{4,2,0,3,1:T(8,128)} %convolution_bitcast_fusion.1), kind=kLoop, calls=%fused_computation.17 | loop fusion | flops 2097152 | bytes 25165824 | tf_op jit(solution)/shard_map/add | solution.py:9
  75.0 3.8 fusion
  80.2 4.1 %maximum_bitcast_fusion = (bf16[32,16,32,1,128]{4,2,0,1,3:T(8,128)(2,1)}, bf16[32,16,32,1,128]{4,2,0,1,3:T(8,128)(2,1)}) fusion(bf16[32,16,16,128]{3,2,0,1:T(8,128)(2,1)S(1)} %fusion.21, bf16[32,16,16,128]{3,2,0,1:T(8,128)(2,1)S(1)} %get-tuple-element.15, bf16[32,16,16,128]{3,2,0,1:T(8,128)(2,1)S(1)} %get-tuple-element.14), kind=kLoop, calls=%fused_computation.18 | loop fusion | flops 16777216 | bytes 14680064 | tf_op jit(solution)/shard_map/stack | solution.py:19
  84.3 63.3 %all-to-all-done = bf16[2,256,32,256]{3,2,0,1:T(8,128)(2,1)} async-done(((bf16[2,256,32,256]{3,2,0,1:T(8,128)(2,1)}), bf16[2,256,32,256]{3,2,0,1:T(8,128)(2,1)}, u32[]{:S(2)}, u32[]{:S(2)}) %all-to-all-start) | async-done | bytes 8388640 | tf_op jit(solution)/shard_map/all_to_all | solution.py:54
  147.6 8.1 %copy.36 = bf16[2,16,16,32,256]{4,3,2,0,1:T(8,128)(2,1)} copy(bf16[2,16,16,32,256]{4,3,0,2,1:T(8,128)(2,1)} %bitcast.8) | data formatting | bytes 16777216 | tf_op jit(solution)/shard_map/all_to_all | solution.py:54
  155.6 11.5 %fusion.10 = f32[32,256,2,128]{1,3,2,0:T(8,128)} fusion(bf16[32,16,32,256,1]{3,2,1,4,0:T(8,128)(2,1)} %bitcast.64, bf16[32,16,32,1,128]{4,2,0,1,3:T(8,128)(2,1)} %get-tuple-element.19, bf16[32,16,32,1,128]{4,2,0,1,3:T(8,128)(2,1)} %get-tuple-element.18), kind=kOutput, calls=%fused_computation.24 | convolution fusion | flops 2151677952 | bytes 25165824 | tf_op jit(solution)/shard_map/ijrk,ijrcs->ikcs/dot_general | solution.py:28
  167.1 8.9 %copy.38 = f32[32,256,2,128]{3,1,0,2:T(8,128)} copy(f32[32,256,2,128]{1,3,2,0:T(8,128)} %fusion.10) | data formatting | bytes 16777216 | tf_op jit(solution)/shard_map/ijrk,ijrcs->ikcs/dot_general | solution.py:28
  176.1 86.2 %reduce-scatter.3.cloned.1.call-done = f32[512,2,128]{2,0,1:T(8,128)} async-done(((f32[8192,2,128]{2,0,1:T(8,128)}), f32[512,2,128]{2,0,1:T(8,128)}) %reduce-scatter.3.cloned.1.call-update) | async-done | bytes 524304 | tf_op jit(solution)/shard_map/reduce_scatter | solution.py:56
  262.2 1.8 fusion.23
  264.4 51.5 %all-gather.5.cloned.1.call-done = bf16[8192,2,128]{2,0,1:T(8,128)(2,1)} async-done(((bf16[512,2,128]{2,0,1:T(8,128)(2,1)}), bf16[8192,2,128]{2,0,1:T(8,128)(2,1)}) %all-gather.5.cloned.1.call-update) | async-done | bytes 4194320 | tf_op jit(solution)/shard_map/all_gather | solution.py:59
  315.8 12.7 %convolution_bitcast_fusion = f32[32,16,32,2,128]{4,2,1,3,0:T(8,128)} fusion(bf16[32,16,32,256,1]{3,2,1,4,0:T(8,128)(2,1)} %bitcast.65, bf16[32,256,2,128,1]{3,1,0,2,4:T(8,128)(2,1)} %bitcast.68), kind=kOutput, calls=%fused_computation | convolution fusion | flops 2147483648 | bytes 29360128 | tf_op jit(solution)/shard_map/ijrk,ikcs->ijrcs/dot_general | solution.py:34
  328.6 6.7 %fusion.8 = (bf16[32,16,16,1,128]{4,2,1,3,0:T(8,128)(2,1)S(1)}, bf16[32,16,16,1,128]{4,2,1,3,0:T(8,128)(2,1)S(1)}) fusion(f32[32,16,32,2,128]{4,2,1,3,0:T(8,128)} %convolution_bitcast_fusion), kind=kLoop, calls=%fused_computation.15 | loop fusion | flops 4194304 | bytes 20971520 | tf_op jit(solution)/shard_map/convert
  335.3 1.4 maximum_multiply_fusion.1
  336.7 1.3 slice_bitcast_fusion
  338.3 4.2 %maximum_bitcast_fusion.2 = (bf16[32,16,32,1,128]{4,2,1,0,3:T(8,128)(2,1)}, bf16[32,16,32,1,128]{4,2,1,0,3:T(8,128)(2,1)}) fusion(bf16[32,16,16,128]{3,2,1,0:T(8,128)(2,1)S(1)} %fusion.22, bf16[32,16,16,128]{3,2,1,0:T(8,128)(2,1)S(1)} %get-tuple-element.13, bf16[32,16,16,128]{3,2,1,0:T(8,128)(2,1)S(1)} %get-tuple-element.12), kind=kLoop, calls=%fused_computation.21 | loop fusion | flops 16777216 | bytes 14680064 | tf_op jit(solution)/shard_map/stack | solution.py:19
  342.4 10.3 %fusion.13 = f32[16,256,2,128]{1,3,2,0:T(8,128)} fusion(bf16[32,16,32,1,128]{4,2,1,0,3:T(8,128)(2,1)} %get-tuple-element.17, bf16[32,16,32,1,128]{4,2,1,0,3:T(8,128)(2,1)} %get-tuple-element.16, bf16[32,16,32,256]{3,2,1,0:T(8,128)(2,1)} %param.7), kind=kOutput, calls=%fused_computation.25 | convolution fusion | flops 2151677952 | bytes 20971520 | tf_op jit(solution)/shard_map/ijrk,ijrcs->jkcs/dot_general | solution.py:40
  352.7 5.4 %copy.45 = f32[16,256,2,128]{3,1,0,2:T(8,128)} copy(f32[16,256,2,128]{1,3,2,0:T(8,128)} %fusion.13) | data formatting | bytes 8388608 | tf_op jit(solution)/shard_map/ijrk,ijrcs->jkcs/dot_general | solution.py:40
  358.1 1.2 copy.46
  359.3 36.5 %reduce-scatter.5.cloned.1.call-done = f32[512,2,128]{2,0,1:T(8,128)} async-done(((f32[4096,2,128]{2,0,1:T(8,128)}), f32[512,2,128]{2,0,1:T(8,128)}) %reduce-scatter.5.cloned.1.call-update) | async-done | bytes 524304 | tf_op jit(solution)/shard_map/reduce_scatter | solution.py:62
  395.9 2.2 copy.47
  (20 shorter events, 3.0 us)
Async XLA Ops:
  15.2 8.2 %copy-start = (bf16[512,2,128]{2,1,0:T(2,128)(2,1)S(1)}, bf16[512,2,128]{2,1,0:T(2,128)(2,1)}, u32[]{:S(2)}) copy-start(bf16[512,2,128]{2,1,0:T(2,128)(2,1)} %param.5) | copy-start | bytes 786436
  15.2 9.1 %copy-start.2 = (s32[32,16]{0,1:T(8,128)S(1)}, s32[32,16]{0,1:T(8,128)}, u32[]{:S(2)}) copy-start(s32[32,16]{0,1:T(8,128)} %param.9) | copy-start | bytes 6148
  15.2 132.3 %all-to-all-start = ((bf16[2,256,32,256]{3,2,0,1:T(8,128)(2,1)}), bf16[2,256,32,256]{3,2,0,1:T(8,128)(2,1)}, u32[]{:S(2)}, u32[]{:S(2)}) async-start(bf16[2,256,32,256]{3,2,0,1:T(8,128)(2,1)} %copy.35), calls=%async_computation | async-start | bytes 16777216 | tf_op jit(solution)/shard_map/all_to_all | solution.py:54
  23.4 30.1 %all-gather.3.cloned.1.call-start = ((), (), s32[]{:S(2)}) async-start(), calls=%async_computation.3 | async-start | bytes 2359296 | tf_op jit(solution)/shard_map/all_gather | solution.py:51
  24.2 238.0 %reduce-scatter.3.cloned.1.call-start = ((), (), s32[]{:S(2)}) async-start(), calls=%async_computation.4 | async-start | bytes 8912896 | tf_op jit(solution)/shard_map/reduce_scatter | solution.py:56
  176.0 86.2 %copy-start.1 = (bf16[512,2,128]{2,1,0:T(2,128)(2,1)S(1)}, bf16[512,2,128]{2,1,0:T(2,128)(2,1)}, u32[]{:S(2)}) copy-start(bf16[512,2,128]{2,1,0:T(2,128)(2,1)} %param.6) | copy-start | bytes 786436
  176.0 139.8 %all-gather.5.cloned.1.call-start = ((), (), s32[]{:S(2)}) async-start(), calls=%async_computation.5 | async-start | bytes 4456448 | tf_op jit(solution)/shard_map/all_gather | solution.py:59
  264.1 131.8 %reduce-scatter.5.cloned.1.call-start = ((), (), s32[]{:S(2)}) async-start(), calls=%async_computation.6 | async-start | bytes 4718592 | tf_op jit(solution)/shard_map/reduce_scatter | solution.py:62
Sparse Core Ops, SparseCore 0:
  26.5 26.9 all-gather.2
  176.2 86.0 reduce-scatter.2
  265.0 50.8 all-gather.4
  358.3 37.5 reduce-scatter.4
where the time goes:
time: 405 us
  waiting for transfers between devices  267 us (66%)
  matrix products  46.6 us (12%)
  local copies, waits for them, and re-layouts  37.1 us (9%)
  other arithmetic  32 us (8%)
  between operations  13.9 us (3%)
  starting transfers between devices  8.52 us (2%)
    reduce_scatter x1, waiting for transfers between devices, body(): lax.psum_scatter(partial_value, 'col', scatter_dimension=0, tiled=True)  86.2 us
    all_to_all x1, waiting for transfers between devices, body(): lax.all_to_all(u_bases, 'col', split_axis=1, concat_axis=0, tiled=True)  63.3 us
    all_gather x1, waiting for transfers between devices, body(): lax.all_gather(rounded, 'col', axis=0, tiled=True)  51.5 us
    reduce_scatter x1, waiting for transfers between devices, body(): lax.psum_scatter(column_terms.reshape(-1, 2, sources), 'row', scatter_dim...  36.5 us
    all_gather x1, waiting for transfers between devices, body(): gathered = lax.all_gather(wavefield, 'row', axis=0, tiled=True)  29.1 us
    dot_general x1, matrix products, u_adjoint(): jnp.einsum('ijrk,ikcs->ijrcs', bases, rows, preferred_element_type=jnp.fl...  12.7 us
    unnamed x10, local copies, waits for them, and re-layouts  12.3 us
    dot_general x1, matrix products, v_adjoint(): jnp.einsum('ijrk,jkcs->ijrcs', bases, blocks, preferred_element_type=jnp....  12.1 us
  transfers between devices with their start and end apart: 5, of which 5 were waited for; matrix products, arithmetic and copies ran while one was open for 8% of the time, Pallas kernels for 0%

commit v1 on v0

--- a/solution.py
+++ b/solution.py
@@ -56,7 +56,16 @@
     modelled = lax.psum_scatter(partial_value, "col", scatter_dimension=0, tiled=True)
     residual = modelled - recorded.astype(jnp.float32)
     rounded = residual.astype(jnp.bfloat16)
-    whole_rows = lax.all_gather(rounded, "col", axis=0, tiled=True).reshape(-1, tile, 2, sources)
+
+    def compute_stops_all_up(local_array, array_axis):
+        sides = []
+        for _ in range(lax.axis_size("col")):
+            sides.append(local_array)
+        z_new = jnp.stack(sides, 0)
+        g_now = lax.all_to_all(z_new, concat_axis=0, split_axis=0, axis_name="col")
+        return jnp.concatenate(g_now, array_axis)
+
+    whole_rows = compute_stops_all_up(rounded, 0).reshape(-1, tile, 2, sources)
     back = u_adjoint(local_left, whole_rows)
     column_terms = v_apply(v_bases, back, mask)
     gradient = lax.psum_scatter(

time: 405 us -> 424 us (1.047)
  local copies, waits for them, and re-layouts: 37.1 us -> 44.7 us
  waiting for transfers between devices: 267 us -> 273 us
  starting transfers between devices: 8.52 us -> 13.4 us
    all_to_all x0 -> x1, waiting for transfers between devices: none -> 59 us  [compute_stops_all_up(): g_now = lax.all_to_all(z_new, concat_axis=0, split_axis=0, axis_name='col')]
    all_gather x1 -> x0, waiting for transfers between devices: 51.5 us -> none  [body(): lax.all_gather(rounded, 'col', axis=0, tiled=True)]
    all_to_all x0 -> x1, starting transfers between devices: none -> 4.96 us  [compute_stops_all_up(): g_now = lax.all_to_all(z_new, concat_axis=0, split_axis=0, axis_name='col')]
    all_to_all x0 -> x1, local copies, waits for them, and re-layouts: none -> 4.61 us  [compute_stops_all_up(): g_now = lax.all_to_all(z_new, concat_axis=0, split_axis=0, axis_name='col')]
where the time goes in v1:
time: 424 us; the launch traced here: 423 us
  waiting for transfers between devices  273 us (64%)
  matrix products  46.7 us (11%)
  local copies, waits for them, and re-layouts  44.7 us (11%)
  other arithmetic  31.2 us (7%)
  between operations  13.9 us (3%)
  starting transfers between devices  13.4 us (3%)
    reduce_scatter x1, waiting for transfers between devices, body(): lax.psum_scatter(partial_value, 'col', scatter_dimension=0, tiled=True)  86.3 us
    all_to_all x1, waiting for transfers between devices, body(): lax.all_to_all(u_bases, 'col', split_axis=1, concat_axis=0, tiled=True)  63.3 us
    all_to_all x1, waiting for transfers between devices, compute_stops_all_up(): g_now = lax.all_to_all(z_new, concat_axis=0, split_axis=0, axis_name='col')  59 us
    reduce_scatter x1, waiting for transfers between devices, body(): lax.psum_scatter(column_terms.reshape(-1, 2, sources), 'row', scatter_dim...  35.4 us
    all_gather x1, waiting for transfers between devices, body(): gathered = lax.all_gather(wavefield, 'row', axis=0, tiled=True)  29.1 us
    dot_general x1, matrix products, u_adjoint(): jnp.einsum('ijrk,ikcs->ijrcs', bases, rows, preferred_element_type=jnp.fl...  12.7 us
    unnamed x10, local copies, waits for them, and re-layouts  12.3 us
    dot_general x1, matrix products, v_adjoint(): jnp.einsum('ijrk,jkcs->ijrcs', bases, blocks, preferred_element_type=jnp....  12.1 us
  transfers between devices with their start and end apart: 5, of which 5 were waited for; matrix products, arithmetic and copies ran while one was open for 8% of the time, Pallas kernels for 0%

profile of v1, /device:TPU:0, one launch (start us, length us, event | category | flops | bytes accessed | tf_op | source)
XLA Modules:
  0.0 422.9 jit_solution(13142162256562012293)
XLA Ops:
  7.2 8.1 %copy.35 = bf16[2,256,32,256]{3,2,0,1:T(8,128)(2,1)} copy(bf16[2,256,32,256]{3,2,1,0:T(8,128)(2,1)} %param.8) | data formatting | bytes 16777216 | tf_op args[3]
  15.2 8.2 %all-to-all-start = ((bf16[2,256,32,256]{3,2,0,1:T(8,128)(2,1)}), bf16[2,256,32,256]{3,2,0,1:T(8,128)(2,1)}, u32[]{:S(2)}, u32[]{:S(2)}) async-start(bf16[2,256,32,256]{3,2,0,1:T(8,128)(2,1)} %copy.35), calls=%async_computation | async-start | bytes 16777216 | tf_op jit(solution)/shard_map/all_to_all | solution.py:54
  24.4 29.1 %all-gather.2.cloned.1.call-done = bf16[4096,2,128]{2,0,1:T(8,128)(2,1)} async-done(((bf16[512,2,128]{2,0,1:T(8,128)(2,1)}), bf16[4096,2,128]{2,0,1:T(8,128)(2,1)}) %all-gather.2.cloned.1.call-update) | async-done | bytes 2097168 | tf_op jit(solution)/shard_map/all_gather | solution.py:51
  53.5 12.1 %convolution_bitcast_fusion.1 = f32[32,16,32,2,128]{4,2,0,3,1:T(8,128)} fusion(bf16[16,256,2,128,1]{3,1,0,2,4:T(8,128)(2,1)} %bitcast.69, bf16[32,16,32,256]{3,2,1,0:T(8,128)(2,1)} %param.7), kind=kOutput, calls=%fused_computation.1 | convolution fusion | flops 2147483648 | bytes 27262976 | tf_op jit(solution)/shard_map/ijrk,jkcs->ijrcs/dot_general | solution.py:23
  65.6 9.4 %slice_add_fusion.1 = (f32[32,16,16,1,128]{4,2,0,3,1:T(8,128)S(1)}, f32[32,16,16,1,128]{4,2,0,3,1:T(8,128)}) fusion(f32[32,16,32,2,128]{4,2,0,3,1:T(8,128)} %convolution_bitcast_fusion.1), kind=kLoop, calls=%fused_computation.17 | loop fusion | flops 2097152 | bytes 25165824 | tf_op jit(solution)/shard_map/add | solution.py:9
  75.0 3.8 fusion
  80.2 4.1 maximum_bitcast_fusion
  84.3 63.3 %all-to-all-done = bf16[2,256,32,256]{3,2,0,1:T(8,128)(2,1)} async-done(((bf16[2,256,32,256]{3,2,0,1:T(8,128)(2,1)}), bf16[2,256,32,256]{3,2,0,1:T(8,128)(2,1)}, u32[]{:S(2)}, u32[]{:S(2)}) %all-to-all-start) | async-done | bytes 8388640 | tf_op jit(solution)/shard_map/all_to_all | solution.py:54
  147.6 8.1 %copy.36 = bf16[2,16,16,32,256]{4,3,2,0,1:T(8,128)(2,1)} copy(bf16[2,16,16,32,256]{4,3,0,2,1:T(8,128)(2,1)} %bitcast.8) | data formatting | bytes 16777216 | tf_op jit(solution)/shard_map/all_to_all | solution.py:54
  155.6 11.5 %fusion.10 = f32[32,256,2,128]{1,3,2,0:T(8,128)} fusion(bf16[32,16,32,256,1]{3,2,1,4,0:T(8,128)(2,1)} %bitcast.64, bf16[32,16,32,1,128]{4,2,0,1,3:T(8,128)(2,1)} %get-tuple-element.19, bf16[32,16,32,1,128]{4,2,0,1,3:T(8,128)(2,1)} %get-tuple-element.18), kind=kOutput, calls=%fused_computation.24 | convolution fusion | flops 2151677952 | bytes 25165824 | tf_op jit(solution)/shard_map/ijrk,ijrcs->ikcs/dot_general | solution.py:28
  167.1 8.9 %copy.38 = f32[32,256,2,128]{3,1,0,2:T(8,128)} copy(f32[32,256,2,128]{1,3,2,0:T(8,128)} %fusion.10) | data formatting | bytes 16777216 | tf_op jit(solution)/shard_map/ijrk,ijrcs->ikcs/dot_general | solution.py:28
  176.1 86.3 %reduce-scatter.3.cloned.1.call-done = f32[512,2,128]{2,0,1:T(8,128)} async-done(((f32[8192,2,128]{2,0,1:T(8,128)}), f32[512,2,128]{2,0,1:T(8,128)}) %reduce-scatter.3.cloned.1.call-update) | async-done | bytes 524304 | tf_op jit(solution)/shard_map/reduce_scatter | solution.py:56
  263.4 2.9 stack.23
  266.4 5.0 %all-to-all-start.1 = ((bf16[16,512,2,128]{3,1,2,0:T(8,128)(2,1)}), bf16[16,512,2,128]{3,1,2,0:T(8,128)(2,1)}, u32[]{:S(2)}, u32[]{:S(2)}) async-start(bf16[16,512,2,128]{3,1,2,0:T(8,128)(2,1)} %stack.23), calls=%async_computation.2 | async-start | bytes 8388608 | tf_op jit(solution)/shard_map/all_to_all | solution.py:65
  271.6 59.0 %all-to-all-done.1 = bf16[16,512,2,128]{3,1,2,0:T(8,128)(2,1)} async-done(((bf16[16,512,2,128]{3,1,2,0:T(8,128)(2,1)}), bf16[16,512,2,128]{3,1,2,0:T(8,128)(2,1)}, u32[]{:S(2)}, u32[]{:S(2)}) %all-to-all-start.1) | async-done | bytes 4194336 | tf_op jit(solution)/shard_map/all_to_all | solution.py:65
  330.6 4.6 %copy.40 = bf16[16,512,2,128]{3,1,0,2:T(8,128)(2,1)} copy(bf16[16,512,2,128]{3,1,2,0:T(8,128)(2,1)} %all-to-all-done.1) | data formatting | bytes 8388608 | tf_op jit(solution)/shard_map/all_to_all | solution.py:65
  335.2 12.7 %convolution_bitcast_fusion = f32[32,16,32,2,128]{4,2,1,3,0:T(8,128)} fusion(bf16[32,16,32,256,1]{3,2,1,4,0:T(8,128)(2,1)} %bitcast.65, bf16[32,256,2,128,1]{3,1,0,2,4:T(8,128)(2,1)} %bitcast.67), kind=kOutput, calls=%fused_computation | convolution fusion | flops 2147483648 | bytes 29360128 | tf_op jit(solution)/shard_map/ijrk,ikcs->ijrcs/dot_general | solution.py:34
  348.0 6.7 %fusion.8 = (bf16[32,16,16,1,128]{4,2,1,3,0:T(8,128)(2,1)S(1)}, bf16[32,16,16,1,128]{4,2,1,3,0:T(8,128)(2,1)S(1)}) fusion(f32[32,16,32,2,128]{4,2,1,3,0:T(8,128)} %convolution_bitcast_fusion), kind=kLoop, calls=%fused_computation.15 | loop fusion | flops 4194304 | bytes 20971520 | tf_op jit(solution)/shard_map/convert
  354.7 1.4 maximum_multiply_fusion.1
  357.7 4.2 maximum_bitcast_fusion.2
  361.8 10.3 %fusion.13 = f32[16,256,2,128]{1,3,2,0:T(8,128)} fusion(bf16[32,16,32,1,128]{4,2,1,0,3:T(8,128)(2,1)} %get-tuple-element.17, bf16[32,16,32,1,128]{4,2,1,0,3:T(8,128)(2,1)} %get-tuple-element.16, bf16[32,16,32,256]{3,2,1,0:T(8,128)(2,1)} %param.7), kind=kOutput, calls=%fused_computation.25 | convolution fusion | flops 2151677952 | bytes 20971520 | tf_op jit(solution)/shard_map/ijrk,ijrcs->jkcs/dot_general | solution.py:40
  372.1 5.4 %copy.46 = f32[16,256,2,128]{3,1,0,2:T(8,128)} copy(f32[16,256,2,128]{1,3,2,0:T(8,128)} %fusion.13) | data formatting | bytes 8388608 | tf_op jit(solution)/shard_map/ijrk,ijrcs->jkcs/dot_general | solution.py:40
  378.8 35.4 %reduce-scatter.5.cloned.1.call-done = f32[512,2,128]{2,0,1:T(8,128)} async-done(((f32[4096,2,128]{2,0,1:T(8,128)}), f32[512,2,128]{2,0,1:T(8,128)}) %reduce-scatter.5.cloned.1.call-update) | async-done | bytes 524304 | tf_op jit(solution)/shard_map/reduce_scatter | solution.py:71
  414.2 2.2 copy.48
  (21 shorter events, 6.6 us)
Async XLA Ops:
  15.2 8.2 %copy-start = (bf16[512,2,128]{2,1,0:T(2,128)(2,1)S(1)}, bf16[512,2,128]{2,1,0:T(2,128)(2,1)}, u32[]{:S(2)}) copy-start(bf16[512,2,128]{2,1,0:T(2,128)(2,1)} %param.5) | copy-start | bytes 786436
  15.2 9.1 %copy-start.2 = (s32[32,16]{0,1:T(8,128)S(1)}, s32[32,16]{0,1:T(8,128)}, u32[]{:S(2)}) copy-start(s32[32,16]{0,1:T(8,128)} %param.9) | copy-start | bytes 6148
  15.2 132.3 %all-to-all-start = ((bf16[2,256,32,256]{3,2,0,1:T(8,128)(2,1)}), bf16[2,256,32,256]{3,2,0,1:T(8,128)(2,1)}, u32[]{:S(2)}, u32[]{:S(2)}) async-start(bf16[2,256,32,256]{3,2,0,1:T(8,128)(2,1)} %copy.35), calls=%async_computation | async-start | bytes 16777216 | tf_op jit(solution)/shard_map/all_to_all | solution.py:54
  23.4 30.1 %all-gather.2.cloned.1.call-start = ((), (), s32[]{:S(2)}) async-start(), calls=%async_computation.4 | async-start | bytes 2359296 | tf_op jit(solution)/shard_map/all_gather | solution.py:51
  24.2 238.1 %reduce-scatter.3.cloned.1.call-start = ((), (), s32[]{:S(2)}) async-start(), calls=%async_computation.5 | async-start | bytes 8912896 | tf_op jit(solution)/shard_map/reduce_scatter | solution.py:56
  176.0 86.3 %copy-start.1 = (bf16[512,2,128]{2,1,0:T(2,128)(2,1)S(1)}, bf16[512,2,128]{2,1,0:T(2,128)(2,1)}, u32[]{:S(2)}) copy-start(bf16[512,2,128]{2,1,0:T(2,128)(2,1)} %param.6) | copy-start | bytes 786436
  266.4 64.3 %all-to-all-start.1 = ((bf16[16,512,2,128]{3,1,2,0:T(8,128)(2,1)}), bf16[16,512,2,128]{3,1,2,0:T(8,128)(2,1)}, u32[]{:S(2)}, u32[]{:S(2)}) async-start(bf16[16,512,2,128]{3,1,2,0:T(8,128)(2,1)} %stack.23), calls=%async_computation.2 | async-start | bytes 8388608 | tf_op jit(solution)/shard_map/all_to_all | solution.py:65
  271.3 142.8 %reduce-scatter.5.cloned.1.call-start = ((), (), s32[]{:S(2)}) async-start(), calls=%async_computation.6 | async-start | bytes 4718592 | tf_op jit(solution)/shard_map/reduce_scatter | solution.py:71
Sparse Core Ops, SparseCore 0:
  26.5 26.9 all-gather.1
  176.2 86.0 reduce-scatter.2
  377.7 36.4 reduce-scatter.4
